TPU v7x, 768 devices: a whole 4x8x12 slice. The times are simulated.
768 devices in a mesh: outer: 96 (over z, x, core), inner: 8 (over y).
Axes of the slice: x: 4, y: 8, z: 12, core: 2. Of those that a mesh axis runs over, the one named last changes fastest.
Arguments:
- query_rows: bfloat16 [196608, 256], P(('outer', 'inner')), may hold values from -6 to 6
- key_rows: bfloat16 [196608, 256], P(('outer', 'inner')), may hold values from -6 to 6
- value_rows: bfloat16 [196608, 256], P(('outer', 'inner')), may hold values from -6 to 6
- grad_output: bfloat16 [196608, 256], P(('outer', 'inner')), may hold values from -6 to 6
Outputs:
- attended: bfloat16 [196608, 256], P(('outer', 'inner'))
- grad_queries: bfloat16 [196608, 256], P(('outer', 'inner'))
- grad_keys: bfloat16 [196608, 256], P(('outer', 'inner'))
- grad_values: bfloat16 [196608, 256], P(('outer', 'inner'))
All inputs are finite; a program needn't handle non-finite values.
Results may differ from a plain program's by a relative error of at most 0.014.
Values may be sent and summed in bfloat16 or wider, within the bound.
A program may use at most 32 MiB of HBM per device.

v0:
```python
import jax
import jax.numpy as jnp
from jax import lax
from jax.sharding import PartitionSpec as P

H = 2
DH = 128


eps = 1e-06


def entering(shard, axis, combine, identity, reverse):
    length, position = (lax.axis_size(axis), lax.axis_index(axis))
    everything = lax.all_gather(shard, axis)
    start = jnp.broadcast_to(jnp.asarray(identity, shard.dtype), shard.shape)

    def hop(k, before):
        at = length - 1 - k if reverse else k
        reached = at > position if reverse else at < position
        new = combine(before, everything[at])
        return jnp.where(reached, new, before)

    return lax.fori_loop(0, length, hop, start)


def add_states(earlier, later):
    return earlier + later


def masked_scores(left, right, rows):
    lower = jnp.tril(jnp.ones((rows, rows), dtype=bool))
    raw = jnp.einsum("thd,shd->hts", left, right, preferred_element_type=jnp.float32)
    return jnp.where(lower[None], raw, 0.0).astype(jnp.bfloat16)


def group_fold(piece, site_lower):
    own = lax.axis_index("inner")
    zeros = jnp.zeros(piece.shape, jnp.float32)
    if site_lower:
        span_piece = lax.all_gather(piece[None], "inner", axis=0, tiled=True)
        index = jnp.arange(span_piece.shape[0], dtype=jnp.int32)
        wide = span_piece.astype(jnp.float32)
        take = (index < own)[:, None, None, None]
        within = jnp.sum(jnp.where(take, wide, 0.0), axis=0)
        total = jnp.sum(wide, axis=0)
        before = entering(total, "outer", add_states, zeros, False)
    else:
        span_piece = lax.all_gather(piece[None], "inner", axis=0, tiled=True)
        index = jnp.arange(span_piece.shape[0], dtype=jnp.int32)
        wide = span_piece.astype(jnp.float32)
        take = (index > own)[:, None, None, None]
        within = jnp.sum(jnp.where(take, wide, 0.0), axis=0)
        total = jnp.sum(wide, axis=0)
        before = entering(total, "outer", add_states, zeros, True)
    return before + within


def local(query_rows, key_rows, value_rows, grad_output):
    rows = query_rows.shape[0]
    query = query_rows.reshape(rows, H, DH)
    key_blk = key_rows.reshape(rows, H, DH)
    value = value_rows.reshape(rows, H, DH)
    piece = jnp.einsum("thd,the->hde", key_blk, value, preferred_element_type=jnp.float32).astype(
        jnp.bfloat16
    )
    prefix = group_fold(piece, True)
    scores = masked_scores(query, key_blk, rows)
    local_mix = jnp.einsum("hts,she->the", scores, value, preferred_element_type=jnp.float32)
    prefix_round = prefix.astype(jnp.bfloat16)
    mixed = local_mix + jnp.einsum(
        "thd,hde->the", query, prefix_round, preferred_element_type=jnp.float32
    )
    inverse = lax.rsqrt(jnp.mean(mixed * mixed, axis=-1, keepdims=True) + eps)
    normed = mixed * inverse
    attended = normed.astype(jnp.bfloat16)
    grad_float = grad_output.reshape(rows, H, DH).astype(jnp.float32)
    grad_mixed = (
        inverse * (grad_float - normed * jnp.mean(grad_float * normed, axis=-1, keepdims=True))
    ).astype(jnp.bfloat16)
    back_piece = jnp.einsum(
        "thd,the->hde", query, grad_mixed, preferred_element_type=jnp.float32
    ).astype(jnp.bfloat16)
    suffix = group_fold(back_piece, False)
    grad_scores = masked_scores(grad_mixed, value, rows)
    grad_q = jnp.einsum("hts,shd->thd", grad_scores, key_blk, preferred_element_type=jnp.float32)
    grad_q = grad_q + jnp.einsum(
        "the,hde->thd", grad_mixed, prefix_round, preferred_element_type=jnp.float32
    )
    suffix_round = suffix.astype(jnp.bfloat16)
    grad_k = jnp.einsum("hts,thd->shd", grad_scores, query, preferred_element_type=jnp.float32)
    grad_k = grad_k + jnp.einsum(
        "she,hde->shd", value, suffix_round, preferred_element_type=jnp.float32
    )
    grad_v = jnp.einsum("hts,the->she", scores, grad_mixed, preferred_element_type=jnp.float32)
    grad_v = grad_v + jnp.einsum(
        "shd,hde->she", key_blk, suffix_round, preferred_element_type=jnp.float32
    )
    width = H * DH
    return (
        attended.reshape(rows, width),
        grad_q.astype(jnp.bfloat16).reshape(rows, width),
        grad_k.astype(jnp.bfloat16).reshape(rows, width),
        grad_v.astype(jnp.bfloat16).reshape(rows, width),
    )


def solution(mesh):
    in_specs = (
        P(("outer", "inner"), None),
        P(("outer", "inner"), None),
        P(("outer", "inner"), None),
        P(("outer", "inner"), None),
    )
    out_specs = (
        P(("outer", "inner"), None),
        P(("outer", "inner"), None),
        P(("outer", "inner"), None),
        P(("outer", "inner"), None),
    )
    return jax.shard_map(local, mesh=mesh, in_specs=in_specs, out_specs=out_specs, check_vma=False)
```

profile of v0, /device:TPU:1, one launch (start us, length us, event | category | flops | bytes accessed | tf_op | source)
XLA Modules:
  0.0 519.4 jit_solution(12682813269990343703)
XLA Ops:
  7.3 1.0 copy.86
  8.5 22.5 %all-gather = bf16[16,128,128]{2,1,0:T(8,128)(2,1)S(1)} all-gather(bf16[2,128,128]{2,1,0:T(8,128)(2,1)S(1)} %convolution_convert_fusion.1), channel_id=2, replica_groups=mesh['outer'=96,'inner'=8] {'inner'}, dimensions={0}, use_global_device_ids=true | all-gather | bytes 589824 | tf_op jit(solution)/shard_map/all_gather | solution.py:41
  32.0 1.0 copy.59
  33.0 1.0 copy.37
  34.0 1.2 fusion
  35.2 136.4 %all-gather.7.cloned.1.call-done = f32[192,128,128]{2,1,0:T(8,128)} async-done(((f32[2,128,128]{2,1,0:T(8,128)}), f32[192,128,128]{2,1,0:T(8,128)}) %all-gather.7.cloned.1.call-update) | async-done | bytes 12582928 | tf_op jit(solution)/shard_map/all_gather | solution.py:15
  171.6 93.4 %while.30 = (s32[]{:T(128)}, f32[2,128,128]{2,1,0:T(8,128)S(1)}, s32[]{:T(128)}, f32[96,2,128,128]{3,2,1,0:T(8,128)}, s32[]{:T(128)}, /*index=5*/s32[]{:T(128)}) while((s32[]{:T(128)}, f32[2,128,128]{2,1,0:T(8,128)S(1)}, s32[]{:T(128)}, f32[96,2,128,128]{3,2,1,0:T(8,128)}, s32[]{:T(128)}, /*index=5*/s32[]{:T(128)}) %tuple.88), condition=%wide.region_2.3_spmd.clone, body=%wide.region_1.2_spmd.clone.sunk | while | flops 98308 | bytes 393309 | solution.py:24
  172.6 0.9 add_select_fusion.4
  173.5 0.9 add_select_fusion.4
  174.5 0.9 add_select_fusion.4
  175.5 0.9 add_select_fusion.4
  176.5 0.9 add_select_fusion.4
  177.4 0.9 add_select_fusion.4
  178.4 0.9 add_select_fusion.4
  179.4 0.9 add_select_fusion.4
  180.3 0.9 add_select_fusion.4
  181.3 0.9 add_select_fusion.4
  182.3 0.9 add_select_fusion.4
  183.3 0.9 add_select_fusion.4
  184.2 0.9 add_select_fusion.4
  185.2 0.9 add_select_fusion.4
  266.0 20.5 %all-gather.2 = bf16[16,128,128]{2,1,0:T(8,128)(2,1)S(1)} all-gather(bf16[2,128,128]{2,1,0:T(8,128)(2,1)S(1)} %copy.44), channel_id=4, replica_groups=mesh['outer'=96,'inner'=8] {'inner'}, dimensions={0}, use_global_device_ids=true | all-gather | bytes 589824 | tf_op jit(solution)/shard_map/all_gather | solution.py:49
  289.8 126.6 %all-gather.9.cloned.1.call-done = f32[192,128,128]{2,1,0:T(8,128)} async-done(((f32[2,128,128]{2,1,0:T(8,128)}), f32[192,128,128]{2,1,0:T(8,128)}) %all-gather.9.cloned.1.call-update) | async-done | bytes 12582928 | tf_op jit(solution)/shard_map/all_gather | solution.py:15
  416.4 94.0 %while.31 = (s32[]{:T(128)}, f32[2,128,128]{2,1,0:T(8,128)S(1)}, s32[]{:T(128)}, f32[96,2,128,128]{3,2,1,0:T(8,128)}, s32[]{:T(128)}, /*index=5*/s32[]{:T(128)}, s32[]{:T(128)}, s32[]{:T(128)}) while((s32[]{:T(128)}, f32[2,128,128]{2,1,0:T(8,128)S(1)}, s32[]{:T(128)}, f32[96,2,128,128]{3,2,1,0:T(8,128)}, s32[]{:T(128)}, ...), condition=%wide.region_8.9_spmd.clone, body=%wide.region_7.8_spmd.clone.sunk | while | flops 98312 | bytes 393371 | solution.py:24
  (215 shorter events, 176.6 us)
Async XLA Ops:
  7.2 1.1 copy-start
  7.2 503.4 %copy-start.1 = (bf16[256,256]{1,0:T(8,128)(2,1)S(1)}, bf16[256,256]{1,0:T(8,128)(2,1)}, u32[]{:S(2)}) copy-start(bf16[256,256]{1,0:T(8,128)(2,1)} %param.9) | copy-start | bytes 393220
  7.2 164.4 %all-gather.7.cloned.1.call-start = ((), (), s32[]{:S(2)}) async-start(), calls=%async_computation | async-start | bytes 12713984 | tf_op jit(solution)/shard_map/all_gather | solution.py:15
  31.9 384.5 %all-gather.9.cloned.1.call-start = ((), (), s32[]{:S(2)}) async-start(), calls=%async_computation.1 | async-start | bytes 12713984 | tf_op jit(solution)/shard_map/all_gather | solution.py:15
Sparse Core Ops, SparseCore 0:
  32.0 139.5 all-gather.6
  287.5 128.8 all-gather.8
where the time goes:
time: 523 us; the launch traced here: 519 us
  waiting for transfers between devices  263 us (50%)
  other arithmetic  184 us (35%)
  blocking collectives  43 us (8%)
  between operations  14.3 us (3%)
  local copies, waits for them, and re-layouts  6.22 us (1%)
    all_gather x2, waiting for transfers between devices, entering(): everything = lax.all_gather(shard, axis)  263 us
    select_n x192, other arithmetic, hop(): return jnp.where(reached, new, before)  182 us
    all_gather x2, blocking collectives, group_fold(): span_piece = lax.all_gather(piece[None], 'inner', axis=0, tiled=True)  43 us
  transfers between devices with their start and end apart: 2, of which 2 were waited for; matrix products, arithmetic and copies ran while one was open for 1% of the time, Pallas kernels for 0%

commit v1 on v0

v1 whole, which is shorter than its diff:
```python
import functools

import jax
import jax.numpy as jnp
from jax import lax
from jax.experimental import pallas as pl
from jax.experimental.pallas import tpu as pltpu
from jax.sharding import PartitionSpec as P

H = 2
DH = 128
X = 4
C = 2
eps = 1e-06
MESH = pl.DeviceIdType.MESH
F32 = jnp.float32
BF16 = jnp.bfloat16


def mm(a, b):
    return lax.dot_general(a, b, (((1,), (0,)), ((), ())), preferred_element_type=F32)


def mm_nt(a, b):
    return lax.dot_general(a, b, (((1,), (1,)), ((), ())), preferred_element_type=F32)


def mm_tn(a, b):
    return lax.dot_general(a, b, (((0,), (0,)), ((), ())), preferred_element_type=F32)


def kernel(
    Z,
    Y,
    q_ref,
    k_ref,
    v_ref,
    g_ref,
    att_ref,
    gq_ref,
    gk_ref,
    gv_ref,
    piece,
    inbox,
    xbox,
    zbox,
    outbox,
    state,
    scores,
    mix,
    acc_k,
    acc_v,
    a_sem,
    x_sem,
    r_sem,
    z_send,
    z_recv,
):
    J = C * Y
    rows = (H * DH) // J
    tokens = q_ref.shape[0]
    outer = lax.axis_index("outer")
    y = lax.axis_index("inner")
    c = lax.rem(outer, C)
    x = lax.rem(outer // C, X)
    z = outer // (C * X)
    me = c * Y + y

    def device(zz, xx, cc, yy):
        return ((zz * X + xx) * C + cc, yy)

    def far_first(n):
        return sorted(range(1, n), key=lambda d: -min(d, n - d))

    peers = []
    for d in far_first(Y) + [0]:
        for e in range(C):
            if d or e:
                cc, yy = lax.rem(c + e, C), lax.rem(y + d, Y)
                peers.append((cc * Y + yy, device(z, x, cc, yy)))
    x_peers = [device(z, lax.rem(x + d, X), c, y) for d in far_first(X)]
    z_peers = [(lax.rem(z + d, Z), device(lax.rem(z + d, Z), x, c, y)) for d in far_first(Z)]

    barrier = pltpu.get_barrier_semaphore()
    everyone = [p for _, p in z_peers] + x_peers + [p for _, p in peers]
    for p in everyone:
        pl.semaphore_signal(barrier, inc=1, device_id=p, device_id_type=MESH)

    def part(ref, h):
        return ref[:, h * DH : (h + 1) * DH]

    def chunk(j):
        return pl.ds(pl.multiple_of(j * rows, rows), rows)

    lower = lax.broadcasted_iota(jnp.int32, (tokens, tokens), 0) >= lax.broadcasted_iota(
        jnp.int32, (tokens, tokens), 1
    )

    def spread(s):
        copies = []
        for j, p in peers:
            copy = pltpu.make_async_remote_copy(
                src_ref=piece.at[s, chunk(j)],
                dst_ref=inbox.at[s, me],
                send_sem=a_sem.at[s, 0],
                recv_sem=a_sem.at[s, 1],
                device_id=p,
                device_id_type=MESH,
            )
            copy.start()
        inbox[s, me] = piece[s, chunk(me)]

    def all_of(ref, sem):
        pltpu.make_async_copy(ref, ref, sem).wait()

    def carry(s):
        forward = s == 0
        all_of(inbox.at[s, pl.ds(0, J - 1)], a_sem.at[s, 1])
        run = jnp.zeros((rows, DH), F32)
        enter = [None] * J
        for j in range(J) if forward else reversed(range(J)):
            enter[j] = run
            run = run + inbox[s, j].astype(F32)
        xbox[s, x] = run
        for p in x_peers:
            pltpu.make_async_remote_copy(
                src_ref=xbox.at[s, x],
                dst_ref=xbox.at[s, x],
                send_sem=x_sem.at[s, 0],
                recv_sem=x_sem.at[s, 1],
                device_id=p,
                device_id_type=MESH,
            ).start()
        all_of(xbox.at[s, pl.ds(0, X - 1)], x_sem.at[s, 1])
        before = jnp.zeros((rows, DH), F32)
        total = jnp.zeros((rows, DH), F32)
        for i in range(X):
            term = xbox[s, i]
            total = total + term
            before = before + jnp.where(i < x if forward else i > x, term, 0.0)
        zbox[s, z] = total.astype(zbox.dtype)
        for zz, p in z_peers:

            @pl.when(zz > z if forward else zz < z)
            def _():
                pltpu.make_async_remote_copy(
                    src_ref=zbox.at[s, z],
                    dst_ref=zbox.at[s, z],
                    send_sem=z_send.at[s, zz],
                    recv_sem=z_recv.at[s, z],
                    device_id=p,
                    device_id_type=MESH,
                ).start()

        def take(i, sofar):
            pltpu.make_async_copy(zbox.at[s, i], zbox.at[s, i], z_recv.at[s, i]).wait()
            return sofar + zbox[s, i].astype(F32)

        before = lax.fori_loop(0 if forward else z + 1, z if forward else Z, take, before)
        for j in range(J):
            outbox[s, j] = (enter[j] + before).astype(BF16)
        for j, p in peers:
            pltpu.make_async_remote_copy(
                src_ref=outbox.at[s, j],
                dst_ref=state.at[s, chunk(me)],
                send_sem=r_sem.at[s, 0],
                recv_sem=r_sem.at[s, 1],
                device_id=p,
                device_id_type=MESH,
            ).start()
        state[s, chunk(me)] = outbox[s, me]

    def arrive(s):
        all_of(outbox.at[s, pl.ds(0, J - 1)], r_sem.at[s, 1])

    def drain(s):
        forward = s == 0
        all_of(inbox.at[s, pl.ds(0, J - 1)], a_sem.at[s, 0])
        all_of(xbox.at[s, pl.ds(0, X - 1)], x_sem.at[s, 0])
        all_of(outbox.at[s, pl.ds(0, J - 1)], r_sem.at[s, 0])

        def sent(i, _):
            pltpu.make_async_copy(zbox.at[s, z], zbox.at[s, z], z_send.at[s, i]).wait()
            return 0

        lax.fori_loop(z + 1 if forward else 0, Z if forward else z, sent, 0)

    for h in range(H):
        piece[0, h * DH : (h + 1) * DH] = mm_tn(part(k_ref, h), part(v_ref, h)).astype(BF16)
    pl.semaphore_wait(barrier, len(everyone))
    spread(0)
    for h in range(H):
        raw = mm_nt(part(q_ref, h), part(k_ref, h))
        s_h = jnp.where(lower, raw, 0.0).astype(BF16)
        scores[h] = s_h
        mix[:, h * DH : (h + 1) * DH] = mm(s_h, part(v_ref, h))
    carry(0)
    arrive(0)
    grad_mixed = []
    for h in range(H):
        pref = state[0, h * DH : (h + 1) * DH]
        q = part(q_ref, h)
        mixed = part(mix, h) + mm(q, pref)
        inverse = lax.rsqrt(jnp.mean(mixed * mixed, axis=-1, keepdims=True) + eps)
        normed = mixed * inverse
        att_ref[:, h * DH : (h + 1) * DH] = normed.astype(BF16)
        g = part(g_ref, h).astype(F32)
        gm = (inverse * (g - normed * jnp.mean(g * normed, axis=-1, keepdims=True))).astype(BF16)
        grad_mixed.append(gm)
        piece[1, h * DH : (h + 1) * DH] = mm_tn(q, gm).astype(BF16)
    spread(1)
    for h in range(H):
        gm = grad_mixed[h]
        gs = jnp.where(lower, mm_nt(gm, part(v_ref, h)), 0.0).astype(BF16)
        pref = state[0, h * DH : (h + 1) * DH]
        gq_ref[:, h * DH : (h + 1) * DH] = (mm(gs, part(k_ref, h)) + mm_nt(gm, pref)).astype(BF16)
        acc_k[:, h * DH : (h + 1) * DH] = mm_tn(gs, part(q_ref, h))
        acc_v[:, h * DH : (h + 1) * DH] = mm_tn(scores[h], gm)
    carry(1)
    arrive(1)
    for h in range(H):
        suf = state[1, h * DH : (h + 1) * DH]
        gk_ref[:, h * DH : (h + 1) * DH] = (part(acc_k, h) + mm_nt(part(v_ref, h), suf)).astype(BF16)
        gv_ref[:, h * DH : (h + 1) * DH] = (part(acc_v, h) + mm(part(k_ref, h), suf)).astype(BF16)
    drain(0)
    drain(1)


def solution(mesh):
    Z = mesh.shape["outer"] // (X * C)
    Y = mesh.shape["inner"]
    J = C * Y
    rows = (H * DH) // J
    spec = P(("outer", "inner"), None)

    def local(q, k, v, g):
        tokens, width = q.shape
        vmem = pl.BlockSpec(memory_space=pltpu.VMEM)
        return pl.pallas_call(
            functools.partial(kernel, Z, Y),
            out_shape=[jax.ShapeDtypeStruct((tokens, width), BF16)] * 4,
            in_specs=[vmem] * 4,
            out_specs=[vmem] * 4,
            scratch_shapes=[
                pltpu.VMEM((2, H * DH, DH), BF16),
                pltpu.VMEM((2, J, rows, DH), BF16),
                pltpu.VMEM((2, X, rows, DH), F32),
                pltpu.VMEM((2, Z, rows, DH), BF16),
                pltpu.VMEM((2, J, rows, DH), BF16),
                pltpu.VMEM((2, H * DH, DH), BF16),
                pltpu.VMEM((H, tokens, tokens), BF16),
                pltpu.VMEM((tokens, width), F32),
                pltpu.VMEM((tokens, width), F32),
                pltpu.VMEM((tokens, width), F32),
                pltpu.SemaphoreType.DMA((2, 2)),
                pltpu.SemaphoreType.DMA((2, 2)),
                pltpu.SemaphoreType.DMA((2, 2)),
                pltpu.SemaphoreType.DMA((2, Z)),
                pltpu.SemaphoreType.DMA((2, Z)),
            ],
            compiler_params=pltpu.CompilerParams(collective_id=0, has_side_effects=True),
        )(q, k, v, g)

    return jax.shard_map(
        local, mesh=mesh, in_specs=(spec,) * 4, out_specs=(spec,) * 4, check_vma=False
    )
```

time: 523 us -> 63 us (0.12)
  waiting for transfers between devices: 263 us -> 0 us
  other arithmetic: 184 us -> 0 us
  Pallas kernels: 0 us -> 57.9 us
  blocking collectives: 43 us -> 0 us
  between operations: 14.3 us -> 0.65 us
    all_gather x2 -> x0, waiting for transfers between devices: 263 us -> none  [entering(): everything = lax.all_gather(shard, axis)]
    select_n x192 -> x0, other arithmetic: 182 us -> none  [hop(): return jnp.where(reached, new, before)]
    pallas_call x0 -> x1, Pallas kernels: none -> 57.9 us  [local(): pl.pallas_call(functools.partial(kernel, Z, Y), out_shape=[jax.ShapeDtype...]
    all_gather x2 -> x0, blocking collectives: 43 us -> none  [group_fold(): span_piece = lax.all_gather(piece[None], 'inner', axis=0, tiled=True)]
  transfers between devices with their start and end apart: 2 -> 0, of which waited for: 2 -> 0; matrix products, arithmetic and copies ran while one was open for 1% -> 0% of each run, Pallas kernels for 0% -> 0%
where the time goes in v1:
time: 63 us; the launch traced here: 62.7 us
  Pallas kernels  57.9 us (92%)
  local copies, waits for them, and re-layouts  4.16 us (7%)
  between operations  0.65 us (1%)
    pallas_call x1, Pallas kernels, local(): pl.pallas_call(functools.partial(kernel, Z, Y), out_shape=[jax.ShapeDtype...  57.9 us
    unnamed x10, local copies, waits for them, and re-layouts  4.16 us

profile of v1, /device:TPU:1, one launch (start us, length us, event | category | flops | bytes accessed | tf_op | source)
XLA Modules:
  0.0 62.7 jit_solution(11923459855272985835)
XLA Ops:
  0.6 57.9 %shard_map.75 = (bf16[256,256]{1,0:T(8,128)(2,1)}, bf16[256,256]{1,0:T(8,128)(2,1)}, bf16[256,256]{1,0:T(8,128)(2,1)}, bf16[256,256]{1,0:T(8,128)(2,1)}) custom-call(bf16[256,256]{1,0:T(8,128)(2,1)} %q_ref.1, bf16[256,256]{1,0:T(8,128)(2,1)} %k_ref.1, bf16[256,256]{1,0:T(8,128)(2,1)} %v_ref.1, bf16[256,256]{1,0:T(8,128)(2,1)} %g_ref.1), custom_call_target="tpu_custom_call" | custom-call | tf_op jit(solution)/shard_map/pallas_call | solution.py:239
  58.6 0.0 copy-start.2
  58.6 1.6 %copy.12 = bf16[256,256]{1,0:T(8,128)(2,1)} copy(bf16[256,256]{1,0:T(8,128)(2,1)} %get-tuple-element.8) | data formatting | bytes 262144
  60.2 0.0 copy-done.2
  60.2 0.0 copy-start.1
  60.2 0.7 %copy.13 = bf16[256,256]{1,0:T(8,128)(2,1)} copy(bf16[256,256]{1,0:T(8,128)(2,1)S(1)} %copy-done.2) | data formatting | bytes 262144
  60.8 0.3 copy-done.1
  61.1 0.0 copy-start
  61.1 0.7 %copy.14 = bf16[256,256]{1,0:T(8,128)(2,1)} copy(bf16[256,256]{1,0:T(8,128)(2,1)S(1)} %copy-done.1) | data formatting | bytes 262144
  61.8 0.3 copy-done
  62.1 0.7 %copy.15 = bf16[256,256]{1,0:T(8,128)(2,1)} copy(bf16[256,256]{1,0:T(8,128)(2,1)S(1)} %copy-done) | data formatting | bytes 262144
Async XLA Ops:
  58.6 1.6 %copy-start.2 = (bf16[256,256]{1,0:T(8,128)(2,1)S(1)}, bf16[256,256]{1,0:T(8,128)(2,1)}, u32[]{:S(2)}) copy-start(bf16[256,256]{1,0:T(8,128)(2,1)} %get-tuple-element.9) | copy-start | bytes 393220
  60.2 1.0 %copy-start.1 = (bf16[256,256]{1,0:T(8,128)(2,1)S(1)}, bf16[256,256]{1,0:T(8,128)(2,1)}, u32[]{:S(2)}) copy-start(bf16[256,256]{1,0:T(8,128)(2,1)} %get-tuple-element.10) | copy-start | bytes 393220
  61.1 1.0 %copy-start = (bf16[256,256]{1,0:T(8,128)(2,1)S(1)}, bf16[256,256]{1,0:T(8,128)(2,1)}, u32[]{:S(2)}) copy-start(bf16[256,256]{1,0:T(8,128)(2,1)} %get-tuple-element.11) | copy-start | bytes 393220

commit v2 on v1

--- a/solution.py
+++ b/solution.py
@@ -32,14 +32,18 @@
 def kernel(
     Z,
     Y,
+    q_hbm,
+    k_hbm,
+    v_hbm,
+    g_hbm,
+    att_ref,
+    gq_ref,
+    gk_ref,
+    gv_ref,
     q_ref,
     k_ref,
     v_ref,
     g_ref,
-    att_ref,
-    gq_ref,
-    gk_ref,
-    gv_ref,
     piece,
     inbox,
     xbox,
@@ -55,6 +59,8 @@
     r_sem,
     z_send,
     z_recv,
+    in_sem,
+    reply,
 ):
     J = C * Y
     rows = (H * DH) // J
@@ -79,12 +85,23 @@
                 cc, yy = lax.rem(c + e, C), lax.rem(y + d, Y)
                 peers.append((cc * Y + yy, device(z, x, cc, yy)))
     x_peers = [device(z, lax.rem(x + d, X), c, y) for d in far_first(X)]
-    z_peers = [(lax.rem(z + d, Z), device(lax.rem(z + d, Z), x, c, y)) for d in far_first(Z)]
 
     barrier = pltpu.get_barrier_semaphore()
-    everyone = [p for _, p in z_peers] + x_peers + [p for _, p in peers]
-    for p in everyone:
+    plane = [p for _, p in peers] + x_peers
+    for p in plane:
         pl.semaphore_signal(barrier, inc=1, device_id=p, device_id_type=MESH)
+    loads = {}
+    for i, (name, src, dst) in enumerate(
+        (("k", k_hbm, k_ref), ("v", v_hbm, v_ref), ("q", q_hbm, q_ref), ("g", g_hbm, g_ref))
+    ):
+        loads[name] = pltpu.make_async_copy(src, dst, in_sem.at[i])
+        loads[name].start()
+
+    def greet(zz, _):
+        pl.semaphore_signal(barrier, inc=1, device_id=device(zz, x, c, y), device_id_type=MESH)
+        return 0
+
+    lax.fori_loop(z + 1, Z, greet, 0)
 
     def part(ref, h):
         return ref[:, h * DH : (h + 1) * DH]
@@ -139,18 +156,32 @@
             total = total + term
             before = before + jnp.where(i < x if forward else i > x, term, 0.0)
         zbox[s, z] = total.astype(zbox.dtype)
-        for zz, p in z_peers:
-
-            @pl.when(zz > z if forward else zz < z)
-            def _():
-                pltpu.make_async_remote_copy(
-                    src_ref=zbox.at[s, z],
-                    dst_ref=zbox.at[s, z],
-                    send_sem=z_send.at[s, zz],
-                    recv_sem=z_recv.at[s, z],
-                    device_id=p,
-                    device_id_type=MESH,
-                ).start()
+
+        def send_z(zz):
+            pltpu.make_async_remote_copy(
+                src_ref=zbox.at[s, z],
+                dst_ref=zbox.at[s, z],
+                send_sem=z_send.at[s, zz],
+                recv_sem=z_recv.at[s, z],
+                device_id=device(zz, x, c, y),
+                device_id_type=MESH,
+            ).start()
+
+        if forward:
+
+            def later(zz, _):
+                pl.semaphore_wait(reply.at[zz], 1)
+                send_z(zz)
+                return 0
+
+            lax.fori_loop(z + 1, Z, later, 0)
+        else:
+
+            def earlier(zz, _):
+                send_z(zz)
+                return 0
+
+            lax.fori_loop(0, z, earlier, 0)
 
         def take(i, sofar):
             pltpu.make_async_copy(zbox.at[s, i], zbox.at[s, i], z_recv.at[s, i]).wait()
@@ -185,10 +216,22 @@
 
         lax.fori_loop(z + 1 if forward else 0, Z if forward else z, sent, 0)
 
+    loads["k"].wait()
+    loads["v"].wait()
     for h in range(H):
         piece[0, h * DH : (h + 1) * DH] = mm_tn(part(k_ref, h), part(v_ref, h)).astype(BF16)
-    pl.semaphore_wait(barrier, len(everyone))
+    pl.semaphore_wait(barrier, len(plane) + z)
     spread(0)
+
+    def answer(zz, _):
+        pl.semaphore_signal(
+            reply.at[z], inc=1, device_id=device(zz, x, c, y), device_id_type=MESH
+        )
+        return 0
+
+    lax.fori_loop(0, z, answer, 0)
+    loads["q"].wait()
+    loads["g"].wait()
     for h in range(H):
         raw = mm_nt(part(q_ref, h), part(k_ref, h))
         s_h = jnp.where(lower, raw, 0.0).astype(BF16)
@@ -226,6 +269,16 @@
     drain(1)
 
 
+def flush(*refs):
+    n = len(refs) // 2
+    sem = refs[-1]
+    copies = [pltpu.make_async_copy(refs[i], refs[n + i], sem.at[i]) for i in range(n)]
+    for copy in copies:
+        copy.start()
+    for copy in copies:
+        copy.wait()
+
+
 def solution(mesh):
     Z = mesh.shape["outer"] // (X * C)
     Y = mesh.shape["inner"]
@@ -236,12 +289,15 @@
     def local(q, k, v, g):
         tokens, width = q.shape
         vmem = pl.BlockSpec(memory_space=pltpu.VMEM)
-        return pl.pallas_call(
+        block = pltpu.VMEM((tokens, width), BF16)
+        hbm = pl.BlockSpec(memory_space=pl.ANY)
+        results = pl.pallas_call(
             functools.partial(kernel, Z, Y),
-            out_shape=[jax.ShapeDtypeStruct((tokens, width), BF16)] * 4,
-            in_specs=[vmem] * 4,
+            out_shape=[block] * 4,
+            in_specs=[hbm] * 4,
             out_specs=[vmem] * 4,
-            scratch_shapes=[
+            scratch_shapes=[block] * 4
+            + [
                 pltpu.VMEM((2, H * DH, DH), BF16),
                 pltpu.VMEM((2, J, rows, DH), BF16),
                 pltpu.VMEM((2, X, rows, DH), F32),
@@ -257,9 +313,18 @@
                 pltpu.SemaphoreType.DMA((2, 2)),
                 pltpu.SemaphoreType.DMA((2, Z)),
                 pltpu.SemaphoreType.DMA((2, Z)),
+                pltpu.SemaphoreType.DMA((4,)),
+                pltpu.SemaphoreType.REGULAR((Z,)),
             ],
             compiler_params=pltpu.CompilerParams(collective_id=0, has_side_effects=True),
         )(q, k, v, g)
+        return pl.pallas_call(
+            flush,
+            out_shape=[jax.ShapeDtypeStruct((tokens, width), BF16)] * 4,
+            in_specs=[vmem] * 4,
+            out_specs=[hbm] * 4,
+            scratch_shapes=[pltpu.SemaphoreType.DMA((4,))],
+        )(*[pltpu.with_memory_space_constraint(r, pltpu.VMEM) for r in results])
 
     return jax.shard_map(
         local, mesh=mesh, in_specs=(spec,) * 4, out_specs=(spec,) * 4, check_vma=False

time: 63 us -> 55.1 us (0.87)
  local copies, waits for them, and re-layouts: 4.16 us -> 0 us
  Pallas kernels: 57.9 us -> 54.3 us
    unnamed x10 -> x0, local copies, waits for them, and re-layouts: 4.16 us -> none
    pallas_call x1 -> x2, Pallas kernels: 57.9 us -> 54.3 us  [the longest x1 53.4 us: local(): pl.pallas_call(functools.partial(kernel, Z, Y), out_shape=[block] * 4, in...]
where the time goes in v2:
time: 55.1 us; the launch traced here: 54.9 us
  Pallas kernels  54.3 us (99%)
  between operations  0.64 us (1%)
    pallas_call x1, Pallas kernels, local(): pl.pallas_call(functools.partial(kernel, Z, Y), out_shape=[block] * 4, in...  53.4 us

profile of v2, /device:TPU:1, one launch (start us, length us, event | category | flops | bytes accessed | tf_op | source)
XLA Modules:
  0.0 54.9 jit_solution(16206615581148151020)
XLA Ops:
  0.6 53.4 %shard_map.75 = (bf16[256,256]{1,0:T(8,128)(2,1)S(1)}, bf16[256,256]{1,0:T(8,128)(2,1)S(1)}, bf16[256,256]{1,0:T(8,128)(2,1)S(1)}, bf16[256,256]{1,0:T(8,128)(2,1)S(1)}) custom-call(bf16[256,256]{1,0:T(8,128)(2,1)} %q_hbm.1, bf16[256,256]{1,0:T(8,128)(2,1)} %k_hbm.1, bf16[256,256]{1,0:T(8,128)(2,1)} %v_hbm.1, bf16[256,256]{1,0:T(8,128)(2,1)} %g_hbm.1), custom_call_target="tpu_custom_call" | custom-call | tf_op jit(solution)/shard_map/pallas_call | solution.py:294
  54.1 0.8 %shard_map.76 = (bf16[256,256]{1,0:T(8,128)(2,1)}, bf16[256,256]{1,0:T(8,128)(2,1)}, bf16[256,256]{1,0:T(8,128)(2,1)}, bf16[256,256]{1,0:T(8,128)(2,1)}) custom-call(bf16[256,256]{1,0:T(8,128)(2,1)S(1)} %get-tuple-element.8.refs_0_, bf16[256,256]{1,0:T(8,128)(2,1)S(1)} %get-tuple-element.9.refs_1_, bf16[256,256]{1,0:T(8,128)(2,1)S(1)} %get-tuple-element.10.refs_2_, ...), custom_call_target="tpu_custom_call" | custom-call | tf_op jit(solution)/shard_map/pallas_call | solution.py:321

commit v3 on v2

v3 whole, which is shorter than its diff:
```python
import functools

import jax
import jax.numpy as jnp
from jax import lax
from jax.experimental import pallas as pl
from jax.experimental.pallas import tpu as pltpu
from jax.sharding import PartitionSpec as P

H = 2
DH = 128
X = 4
C = 2
eps = 1e-06
MESH = pl.DeviceIdType.MESH
F32 = jnp.float32
BF16 = jnp.bfloat16


def mm(a, b):
    return lax.dot_general(a, b, (((1,), (0,)), ((), ())), preferred_element_type=F32)


def mm_nt(a, b):
    return lax.dot_general(a, b, (((1,), (1,)), ((), ())), preferred_element_type=F32)


def mm_tn(a, b):
    return lax.dot_general(a, b, (((0,), (0,)), ((), ())), preferred_element_type=F32)


def kernel(
    Z,
    Y,
    q_hbm,
    k_hbm,
    v_hbm,
    g_hbm,
    att_ref,
    gq_ref,
    gk_ref,
    gv_ref,
    q_ref,
    k_ref,
    v_ref,
    g_ref,
    piece1,
    inbox1,
    zbox1,
    enter1,
    outbox1,
    state1,
    piece2,
    inbox2,
    zbox2,
    enter2,
    outbox2,
    state2,
    scores,
    mix,
    acc_k,
    acc_v,
    a_sem,
    r_sem,
    z_send,
    z_recv,
    in_sem,
    reply,
):
    J = X * C * Y
    E = Y // 2
    owners = X * C * E
    tokens = q_ref.shape[0]
    outer = lax.axis_index("outer")
    y = lax.axis_index("inner")
    c = lax.rem(outer, C)
    x = lax.rem(outer // C, X)
    z = outer // (C * X)
    me = (x * C + c) * Y + y
    OW = (0, 1, 2, 3)
    early = functools.reduce(jnp.logical_or, [y == o for o in OW])
    seat = (x * C + c) * E + jnp.clip(sum((y >= o).astype(jnp.int32) for o in OW) - 1, 0, E - 1)

    def device(zz, xx, cc, yy):
        return ((zz * X + xx) * C + cc, yy)

    def far_first(n):
        return sorted(range(1, n), key=lambda d: -min(d, n - d))

    def plane(what):
        def ring(d):
            yy = lax.rem(y + d, Y)
            for dx in far_first(X) + [0]:
                for dc in range(C):
                    if dx or dc or not isinstance(d, int):
                        xx, cc = lax.rem(x + dx, X), lax.rem(c + dc, C)
                        what((xx * C + cc) * Y + yy, device(z, xx, cc, yy))

        def far(t, _):
            ring(jnp.where(lax.rem(t, 2) == 1, Y // 2 - (t + 1) // 2, Y // 2 + t // 2))
            return 0

        lax.fori_loop(0, Y - 1, far, 0)
        ring(0)

    def to_owners(what):
        for yy in (0, 1, 2, 3):
            for dx in far_first(X) + [0]:
                for dc in range(C):
                    xx, cc = lax.rem(x + dx, X), lax.rem(c + dc, C)
                    j, p = (xx * C + cc) * E + OW.index(yy), device(z, xx, cc, yy)
                    if dx or dc:
                        what(j, p)
                    else:

                        @pl.when(y != yy)
                        def _():
                            what(j, p)

    barrier = pltpu.get_barrier_semaphore()

    @pl.when(early)
    def _():
        plane(lambda j, p: pl.semaphore_signal(barrier, inc=1, device_id=p, device_id_type=MESH))

        def greet(zz, _):
            pl.semaphore_signal(barrier, inc=1, device_id=device(zz, x, c, y), device_id_type=MESH)
            return 0

        lax.fori_loop(z + 1, Z, greet, 0)

    loads = {}
    for i, (name, src, dst) in enumerate(
        (("k", k_hbm, k_ref), ("v", v_hbm, v_ref), ("q", q_hbm, q_ref), ("g", g_hbm, g_ref))
    ):
        loads[name] = pltpu.make_async_copy(src, dst, in_sem.at[i])
        loads[name].start()

    def part(ref, h):
        return ref[:, h * DH : (h + 1) * DH]

    lower = lax.broadcasted_iota(jnp.int32, (tokens, tokens), 0) >= lax.broadcasted_iota(
        jnp.int32, (tokens, tokens), 1
    )

    def remote(src, dst, send, recv, p):
        pltpu.make_async_remote_copy(
            src_ref=src, dst_ref=dst, send_sem=send, recv_sem=recv, device_id=p, device_id_type=MESH
        ).start()

    def all_of(ref, sem):
        pltpu.make_async_copy(ref, ref, sem).wait()

    def put(piece, h, value):
        n, rows, _ = piece.shape
        piece[h * n // H : (h + 1) * n // H] = value.astype(BF16).reshape(n // H, rows, DH)

    def got(state, h):
        n = state.shape[0]
        return state[h * n // H : (h + 1) * n // H].reshape(DH, DH)

    def carry(inbox, zbox, enter, outbox, z_send, z_recv, forward):
        total = jnp.sum(inbox[...].astype(F32), axis=0)
        zbox[z] = total.astype(zbox.dtype)

        def send_z(zz, _):
            if forward:
                pl.semaphore_wait(reply.at[zz], 1)
            remote(zbox.at[z], zbox.at[z], z_send.at[zz], z_recv.at[z], device(zz, x, c, y))
            return 0

        lax.fori_loop(z + 1 if forward else 0, Z if forward else z, send_z, 0)
        run = jnp.zeros(total.shape, F32)
        for j in range(J) if forward else reversed(range(J)):
            enter[j] = run
            run = run + inbox[j].astype(F32)

        def take(i, sofar):
            all_of(zbox.at[i], z_recv.at[i])
            return sofar + zbox[i].astype(F32)

        before = lax.fori_loop(
            0 if forward else z + 1, z if forward else Z, take, jnp.zeros(total.shape, F32)
        )
        for j in range(J):
            outbox[j] = (enter[j] + before).astype(BF16)

    def drain_z(zbox, z_send, forward):
        def sent(i, _):
            all_of(zbox.at[z], z_send.at[i])
            return 0

        lax.fori_loop(z + 1 if forward else 0, Z if forward else z, sent, 0)

    loads["k"].wait()
    loads["v"].wait()
    for h in range(H):
        put(piece1, h, mm_tn(part(k_ref, h), part(v_ref, h)))
    pl.semaphore_wait(barrier, jnp.where(early, owners - 1 + z, owners))

    @pl.when(early)
    def _():
        def answer(zz, _):
            pl.semaphore_signal(
                reply.at[z], inc=1, device_id=device(zz, x, c, y), device_id_type=MESH
            )
            return 0

        lax.fori_loop(0, z, answer, 0)

    to_owners(lambda j, p: remote(piece1.at[j], inbox1.at[me], a_sem.at[0, 0], a_sem.at[0, 1], p))

    @pl.when(early)
    def _():
        inbox1[me] = piece1[seat]

    loads["q"].wait()
    loads["g"].wait()
    for h in range(H):
        raw = mm_nt(part(q_ref, h), part(k_ref, h))
        s_h = jnp.where(lower, raw, 0.0).astype(BF16)
        scores[h] = s_h
        mix[:, h * DH : (h + 1) * DH] = mm(s_h, part(v_ref, h))

    @pl.when(early)
    def _():
        all_of(inbox1.at[pl.ds(0, J - 1)], a_sem.at[0, 1])
        carry(inbox1, zbox1, enter1, outbox1, z_send.at[0], z_recv.at[0], True)
        plane(
            lambda j, p: remote(outbox1.at[j], state1.at[seat], r_sem.at[0, 0], r_sem.at[0, 1], p)
        )
        state1[seat] = outbox1[me]
        all_of(state1.at[pl.ds(0, owners - 1)], r_sem.at[0, 1])

    @pl.when(jnp.logical_not(early))
    def _():
        all_of(state1, r_sem.at[0, 1])

    grad_mixed = []
    for h in range(H):
        pref = got(state1, h)
        q = part(q_ref, h)
        mixed = part(mix, h) + mm(q, pref)
        inverse = lax.rsqrt(jnp.mean(mixed * mixed, axis=-1, keepdims=True) + eps)
        normed = mixed * inverse
        att_ref[:, h * DH : (h + 1) * DH] = normed.astype(BF16)
        g = part(g_ref, h).astype(F32)
        gm = (inverse * (g - normed * jnp.mean(g * normed, axis=-1, keepdims=True))).astype(BF16)
        grad_mixed.append(gm)
        put(piece2, h, mm_tn(q, gm))
    plane(lambda j, p: remote(piece2.at[j], inbox2.at[me], a_sem.at[1, 0], a_sem.at[1, 1], p))
    inbox2[me] = piece2[me]
    for h in range(H):
        gm = grad_mixed[h]
        gs = jnp.where(lower, mm_nt(gm, part(v_ref, h)), 0.0).astype(BF16)
        pref = got(state1, h)
        gq_ref[:, h * DH : (h + 1) * DH] = (mm(gs, part(k_ref, h)) + mm_nt(gm, pref)).astype(BF16)
        acc_k[:, h * DH : (h + 1) * DH] = mm_tn(gs, part(q_ref, h))
        acc_v[:, h * DH : (h + 1) * DH] = mm_tn(scores[h], gm)
    all_of(inbox2.at[pl.ds(0, J - 1)], a_sem.at[1, 1])
    carry(inbox2, zbox2, enter2, outbox2, z_send.at[1], z_recv.at[1], False)
    plane(lambda j, p: remote(outbox2.at[j], state2.at[me], r_sem.at[1, 0], r_sem.at[1, 1], p))
    state2[me] = outbox2[me]
    all_of(state2.at[pl.ds(0, J - 1)], r_sem.at[1, 1])
    for h in range(H):
        suf = got(state2, h)
        gk_ref[:, h * DH : (h + 1) * DH] = (part(acc_k, h) + mm_nt(part(v_ref, h), suf)).astype(BF16)
        gv_ref[:, h * DH : (h + 1) * DH] = (part(acc_v, h) + mm(part(k_ref, h), suf)).astype(BF16)

    @pl.when(early)
    def _():
        all_of(piece1.at[pl.ds(0, owners - 1)], a_sem.at[0, 0])
        drain_z(zbox1, z_send.at[0], True)
        all_of(outbox1.at[pl.ds(0, J - 1)], r_sem.at[0, 0])

    @pl.when(jnp.logical_not(early))
    def _():
        all_of(piece1, a_sem.at[0, 0])

    all_of(piece2.at[pl.ds(0, J - 1)], a_sem.at[1, 0])
    drain_z(zbox2, z_send.at[1], False)
    all_of(outbox2.at[pl.ds(0, J - 1)], r_sem.at[1, 0])


def flush(*refs):
    n = len(refs) // 2
    sem = refs[-1]
    copies = [pltpu.make_async_copy(refs[i], refs[n + i], sem.at[i]) for i in range(n)]
    for copy in copies:
        copy.start()
    for copy in copies:
        copy.wait()


def solution(mesh):
    Z = mesh.shape["outer"] // (X * C)
    Y = mesh.shape["inner"]
    J = X * C * Y
    spec = P(("outer", "inner"), None)

    def local(q, k, v, g):
        tokens, width = q.shape
        vmem = pl.BlockSpec(memory_space=pltpu.VMEM)
        def stage(owners):
            rows = (H * DH) // owners
            return [
                pltpu.VMEM((owners, rows, DH), BF16),
                pltpu.VMEM((J, rows, DH), BF16),
                pltpu.VMEM((Z, rows, DH), BF16),
                pltpu.VMEM((J, rows, DH), F32),
                pltpu.VMEM((J, rows, DH), BF16),
                pltpu.VMEM((owners, rows, DH), BF16),
            ]

        block = pltpu.VMEM((tokens, width), BF16)
        hbm = pl.BlockSpec(memory_space=pl.ANY)
        results = pl.pallas_call(
            functools.partial(kernel, Z, Y),
            out_shape=[block] * 4,
            in_specs=[hbm] * 4,
            out_specs=[vmem] * 4,
            scratch_shapes=[block] * 4
            + stage(J // 2)
            + stage(J)
            + [
                pltpu.VMEM((H, tokens, tokens), BF16),
                pltpu.VMEM((tokens, width), F32),
                pltpu.VMEM((tokens, width), F32),
                pltpu.VMEM((tokens, width), F32),
                pltpu.SemaphoreType.DMA((2, 2)),
                pltpu.SemaphoreType.DMA((2, 2)),
                pltpu.SemaphoreType.DMA((2, Z)),
                pltpu.SemaphoreType.DMA((2, Z)),
                pltpu.SemaphoreType.DMA((4,)),
                pltpu.SemaphoreType.REGULAR((Z,)),
            ],
            compiler_params=pltpu.CompilerParams(collective_id=0, has_side_effects=True),
        )(q, k, v, g)
        return pl.pallas_call(
            flush,
            out_shape=[jax.ShapeDtypeStruct((tokens, width), BF16)] * 4,
            in_specs=[vmem] * 4,
            out_specs=[hbm] * 4,
            scratch_shapes=[pltpu.SemaphoreType.DMA((4,))],
        )(*[pltpu.with_memory_space_constraint(r, pltpu.VMEM) for r in results])

    return jax.shard_map(
        local, mesh=mesh, in_specs=(spec,) * 4, out_specs=(spec,) * 4, check_vma=False
    )
```

time: 55.1 us -> 53.8 us (0.976)
  Pallas kernels: 54.3 us -> 53 us
    pallas_call x1, Pallas kernels: 53.4 us -> 52.1 us  [local(): pl.pallas_call(functools.partial(kernel, Z, Y), out_shape=[block] * 4, in...]
where the time goes in v3:
time: 53.8 us; the launch traced here: 53.6 us
  Pallas kernels  53 us (99%)
  between operations  0.64 us (1%)
    pallas_call x1, Pallas kernels, local(): pl.pallas_call(functools.partial(kernel, Z, Y), out_shape=[block] * 4, in...  52.1 us

profile of v3, /device:TPU:1, one launch (start us, length us, event | category | flops | bytes accessed | tf_op | source)
XLA Modules:
  0.0 53.6 jit_solution(14792815153266486254)
XLA Ops:
  0.6 52.1 %shard_map.75 = (bf16[256,256]{1,0:T(8,128)(2,1)S(1)}, bf16[256,256]{1,0:T(8,128)(2,1)S(1)}, bf16[256,256]{1,0:T(8,128)(2,1)S(1)}, bf16[256,256]{1,0:T(8,128)(2,1)S(1)}) custom-call(bf16[256,256]{1,0:T(8,128)(2,1)} %q_hbm.1, bf16[256,256]{1,0:T(8,128)(2,1)} %k_hbm.1, bf16[256,256]{1,0:T(8,128)(2,1)} %v_hbm.1, bf16[256,256]{1,0:T(8,128)(2,1)} %g_hbm.1), custom_call_target="tpu_custom_call" | custom-call | tf_op jit(solution)/shard_map/pallas_call | solution.py:317
  52.8 0.8 %shard_map.76 = (bf16[256,256]{1,0:T(8,128)(2,1)}, bf16[256,256]{1,0:T(8,128)(2,1)}, bf16[256,256]{1,0:T(8,128)(2,1)}, bf16[256,256]{1,0:T(8,128)(2,1)}) custom-call(bf16[256,256]{1,0:T(8,128)(2,1)S(1)} %get-tuple-element.8.refs_0_, bf16[256,256]{1,0:T(8,128)(2,1)S(1)} %get-tuple-element.9.refs_1_, bf16[256,256]{1,0:T(8,128)(2,1)S(1)} %get-tuple-element.10.refs_2_, ...), custom_call_target="tpu_custom_call" | custom-call | tf_op jit(solution)/shard_map/pallas_call | solution.py:339

commit v4 on v3

--- a/solution.py
+++ b/solution.py
@@ -134,7 +134,11 @@
         (("k", k_hbm, k_ref), ("v", v_hbm, v_ref), ("q", q_hbm, q_ref), ("g", g_hbm, g_ref))
     ):
         loads[name] = pltpu.make_async_copy(src, dst, in_sem.at[i])
-        loads[name].start()
+        step = src.shape[0] // 4
+        for t in range(4):
+            pltpu.make_async_copy(
+                src.at[pl.ds(t * step, step)], dst.at[pl.ds(t * step, step)], in_sem.at[i]
+            ).start()
 
     def part(ref, h):
         return ref[:, h * DH : (h + 1) * DH]
@@ -164,10 +168,14 @@
         zbox[z] = total.astype(zbox.dtype)
 
         def send_z(zz, _):
-            if forward:
-                pl.semaphore_wait(reply.at[zz], 1)
             remote(zbox.at[z], zbox.at[z], z_send.at[zz], z_recv.at[z], device(zz, x, c, y))
             return 0
+
+        if forward:
+
+            @pl.when(z < Z - 1)
+            def _():
+                pl.semaphore_wait(reply, Z - 1 - z)
 
         lax.fori_loop(z + 1 if forward else 0, Z if forward else z, send_z, 0)
         run = jnp.zeros(total.shape, F32)
@@ -202,7 +210,7 @@
     def _():
         def answer(zz, _):
             pl.semaphore_signal(
-                reply.at[z], inc=1, device_id=device(zz, x, c, y), device_id_type=MESH
+                reply, inc=1, device_id=device(zz, x, c, y), device_id_type=MESH
             )
             return 0
 
@@ -332,7 +340,7 @@
                 pltpu.SemaphoreType.DMA((2, Z)),
                 pltpu.SemaphoreType.DMA((2, Z)),
                 pltpu.SemaphoreType.DMA((4,)),
-                pltpu.SemaphoreType.REGULAR((Z,)),
+                pltpu.SemaphoreType.REGULAR,
             ],
             compiler_params=pltpu.CompilerParams(collective_id=0, has_side_effects=True),
         )(q, k, v, g)

time: 53.8 us -> 53.8 us (level)
  no operation moved by 1% of the time
where the time goes in v4:
time: 53.8 us; the launch traced here: 53.6 us
  Pallas kernels  53 us (99%)
  between operations  0.64 us (1%)
    pallas_call x1, Pallas kernels, local(): pl.pallas_call(functools.partial(kernel, Z, Y), out_shape=[block] * 4, in...  52.1 us

profile of v4, /device:TPU:1, one launch (start us, length us, event | category | flops | bytes accessed | tf_op | source)
XLA Modules:
  0.0 53.6 jit_solution(1369800839928858729)
XLA Ops:
  0.6 52.1 %shard_map.75 = (bf16[256,256]{1,0:T(8,128)(2,1)S(1)}, bf16[256,256]{1,0:T(8,128)(2,1)S(1)}, bf16[256,256]{1,0:T(8,128)(2,1)S(1)}, bf16[256,256]{1,0:T(8,128)(2,1)S(1)}) custom-call(bf16[256,256]{1,0:T(8,128)(2,1)} %q_hbm.1, bf16[256,256]{1,0:T(8,128)(2,1)} %k_hbm.1, bf16[256,256]{1,0:T(8,128)(2,1)} %v_hbm.1, bf16[256,256]{1,0:T(8,128)(2,1)} %g_hbm.1), custom_call_target="tpu_custom_call" | custom-call | tf_op jit(solution)/shard_map/pallas_call | solution.py:325
  52.8 0.8 %shard_map.76 = (bf16[256,256]{1,0:T(8,128)(2,1)}, bf16[256,256]{1,0:T(8,128)(2,1)}, bf16[256,256]{1,0:T(8,128)(2,1)}, bf16[256,256]{1,0:T(8,128)(2,1)}) custom-call(bf16[256,256]{1,0:T(8,128)(2,1)S(1)} %get-tuple-element.8.refs_0_, bf16[256,256]{1,0:T(8,128)(2,1)S(1)} %get-tuple-element.9.refs_1_, bf16[256,256]{1,0:T(8,128)(2,1)S(1)} %get-tuple-element.10.refs_2_, ...), custom_call_target="tpu_custom_call" | custom-call | tf_op jit(solution)/shard_map/pallas_call | solution.py:347

commit v5 on v4

--- a/solution.py
+++ b/solution.py
@@ -56,6 +56,7 @@
     enter2,
     outbox2,
     state2,
+    flipped,
     scores,
     mix,
     acc_k,
@@ -228,6 +229,7 @@
         raw = mm_nt(part(q_ref, h), part(k_ref, h))
         s_h = jnp.where(lower, raw, 0.0).astype(BF16)
         scores[h] = s_h
+        flipped[h * DH : (h + 1) * DH] = part(q_ref, h).T
         mix[:, h * DH : (h + 1) * DH] = mm(s_h, part(v_ref, h))
 
     @pl.when(early)
@@ -255,7 +257,7 @@
         g = part(g_ref, h).astype(F32)
         gm = (inverse * (g - normed * jnp.mean(g * normed, axis=-1, keepdims=True))).astype(BF16)
         grad_mixed.append(gm)
-        put(piece2, h, mm_tn(q, gm))
+        put(piece2, h, mm(flipped[h * DH : (h + 1) * DH], gm))
     plane(lambda j, p: remote(piece2.at[j], inbox2.at[me], a_sem.at[1, 0], a_sem.at[1, 1], p))
     inbox2[me] = piece2[me]
     for h in range(H):
@@ -331,6 +333,7 @@
             + stage(J // 2)
             + stage(J)
             + [
+                pltpu.VMEM((width, tokens), BF16),
                 pltpu.VMEM((H, tokens, tokens), BF16),
                 pltpu.VMEM((tokens, width), F32),
                 pltpu.VMEM((tokens, width), F32),

time: 53.8 us -> 53.8 us (level)
  no operation moved by 1% of the time
where the time goes in v5:
time: 53.8 us; the launch traced here: 53.6 us
  Pallas kernels  53 us (99%)
  between operations  0.64 us (1%)
    pallas_call x1, Pallas kernels, local(): pl.pallas_call(functools.partial(kernel, Z, Y), out_shape=[block] * 4, in...  52.1 us

profile of v5, /device:TPU:1, one launch (start us, length us, event | category | flops | bytes accessed | tf_op | source)
XLA Modules:
  0.0 53.6 jit_solution(16429117356955160839)
XLA Ops:
  0.6 52.1 %shard_map.75 = (bf16[256,256]{1,0:T(8,128)(2,1)S(1)}, bf16[256,256]{1,0:T(8,128)(2,1)S(1)}, bf16[256,256]{1,0:T(8,128)(2,1)S(1)}, bf16[256,256]{1,0:T(8,128)(2,1)S(1)}) custom-call(bf16[256,256]{1,0:T(8,128)(2,1)} %q_hbm.1, bf16[256,256]{1,0:T(8,128)(2,1)} %k_hbm.1, bf16[256,256]{1,0:T(8,128)(2,1)} %v_hbm.1, bf16[256,256]{1,0:T(8,128)(2,1)} %g_hbm.1), custom_call_target="tpu_custom_call" | custom-call | tf_op jit(solution)/shard_map/pallas_call | solution.py:327
  52.8 0.8 %shard_map.76 = (bf16[256,256]{1,0:T(8,128)(2,1)}, bf16[256,256]{1,0:T(8,128)(2,1)}, bf16[256,256]{1,0:T(8,128)(2,1)}, bf16[256,256]{1,0:T(8,128)(2,1)}) custom-call(bf16[256,256]{1,0:T(8,128)(2,1)S(1)} %get-tuple-element.8.refs_0_, bf16[256,256]{1,0:T(8,128)(2,1)S(1)} %get-tuple-element.9.refs_1_, bf16[256,256]{1,0:T(8,128)(2,1)S(1)} %get-tuple-element.10.refs_2_, ...), custom_call_target="tpu_custom_call" | custom-call | tf_op jit(solution)/shard_map/pallas_call | solution.py:350
